TPU v7x, 32 devices: a whole 2x2x4 slice. The times are simulated.
32 devices in a mesh: dp: 4 (over z), space: 2 (over core), mp: 4 (over y, x).
Axes of the slice: x: 2, y: 2, z: 4, core: 2. Of those that a mesh axis runs over, the one named last changes fastest.
Arguments:
- features: bfloat16 [64, 64, 1024], P(('dp', 'space'), None, 'mp'), parts along dimension 0, may hold values from -6 to 6
- deconv_weight: bfloat16 [4, 512, 1024], P(None, 'mp'), may hold values from -0.1875 to 0.1875
- deconv_bias: float32 [512], P('mp'), may hold values from -3 to 3
- lateral_eight: bfloat16 [256, 512], P('mp'), may hold values from -0.25 to 0.25
- lateral_coarse: bfloat16 [2, 256, 1024], P(None, 'mp'), may hold values from -0.1875 to 0.1875
- output_conv: bfloat16 [3, 256, 9, 256], P(None, 'mp'), may hold values from -0.125 to 0.125
- norm_gain: float32 [6, 256], replicated, may hold values from 0.1 to 1.9
- norm_shift: float32 [6, 256], replicated, may hold values from -3 to 3
Outputs:
- level_eight: bfloat16 [256, 16384], P('mp', ('dp', 'space')), parts along dimension 1
- level_sixteen: bfloat16 [256, 4096], P('mp', ('dp', 'space')), parts along dimension 1
- level_thirty: bfloat16 [256, 1024], P('mp', ('dp', 'space')), parts along dimension 1
- level_sixty: bfloat16 [256, 256], P('mp', ('dp', 'space')), parts along dimension 1
There are 4 independent parts, one for each index of `dp`. A program takes and returns all parts, laid end to end along the dimension named above; an argument that names none is the same for every part. Nothing has to cross between parts.
All inputs are finite; a program needn't handle non-finite values.
Results may differ from a plain program's by a relative error of at most 0.015.
Values may be sent and summed in bfloat16 or wider, within the bound.
A program may use at most 64 MiB of HBM per device.

v0:
```python
import jax
import jax.numpy as jnp
from jax import lax
from jax.sharding import PartitionSpec as P

EPSILON = 1e-06


def extended(block, sides, width):
    for axis, dim in sides:
        count = lax.axis_size(axis)
        forward = [(i, i + 1) for i in range(count - 1)]
        backward = [(target, source) for source, target in forward]
        low = lax.ppermute(
            lax.slice_in_dim(block, block.shape[dim] - width, None, axis=dim), axis, forward
        )
        high = lax.ppermute(lax.slice_in_dim(block, 0, width, axis=dim), axis, backward)
        block = jnp.concatenate([low, block, high], axis=dim)
    return block


def pool_pairs(values):
    height, width, depth = values.shape
    return jnp.max(values.reshape(height // 2, 2, width // 2, 2, depth), axis=(1, 3))


def contract_last(weight_rows, data):
    return lax.dot_general(
        weight_rows, data, (((1,), (1,)), ((), ())), preferred_element_type=jnp.float32
    )


def apply_norm(values, sums, squares, neck_width, gain_row, shift_row):
    floats = values.astype(jnp.float32)
    center = (sums / neck_width)[None, :]
    spread = (squares / neck_width)[None, :] - center * center
    scaled = (floats - center) * lax.rsqrt(spread + EPSILON)
    return (scaled * gain_row[:, None] + shift_row[:, None]).astype(jnp.bfloat16)


def cell_moments(values):
    floats = values.astype(jnp.float32)
    return (jnp.sum(floats, axis=0), jnp.sum(floats * floats, axis=0))


def conv_taps(totals, padded, weight, height, width):
    depth = padded.shape[0]
    for tap_index in range(9):
        row_off = tap_index // 3
        col_off = tap_index % 3
        window = padded[:, row_off : row_off + height, col_off : col_off + width].reshape(
            depth, height * width
        )
        rows_used = weight[:, tap_index, :]
        totals = totals + jnp.dot(rows_used, window, preferred_element_type=jnp.float32)
    return totals


def pyramid_level(lateral, height, width, level_index, output_conv, norm_gain, norm_shift):
    local_ch = lateral.shape[0]
    neck_width = local_ch * lax.axis_size("mp")
    own_first = lax.axis_index("mp") * local_ch
    weight = output_conv[level_index]
    initial = jnp.zeros((local_ch, height * width), jnp.float32)
    gathered = lax.all_gather(lateral, "mp", axis=0, tiled=True)
    sums, squares = cell_moments(gathered)
    normed = apply_norm(
        gathered, sums, squares, neck_width, norm_gain[2 * level_index], norm_shift[2 * level_index]
    )
    rimmed = extended(normed.reshape(neck_width, height, width), (("space", 1),), 1)
    padded = jnp.pad(rimmed, ((0, 0), (0, 0), (1, 1)))
    conv_out = conv_taps(initial, padded, weight, height, width)
    convolved = conv_out.astype(jnp.bfloat16)
    sums, squares = lax.psum(cell_moments(convolved), "mp")
    gain_row = lax.dynamic_slice_in_dim(norm_gain[2 * level_index + 1], own_first, local_ch, 0)
    shift_row = lax.dynamic_slice_in_dim(norm_shift[2 * level_index + 1], own_first, local_ch, 0)
    return apply_norm(convolved, sums, squares, neck_width, gain_row, shift_row)


def channel_pyramid(
    features,
    deconv_weight,
    deconv_bias,
    lateral_eight,
    lateral_coarse,
    output_conv,
    norm_gain,
    norm_shift,
):
    row_count, col_count, _ = features.shape
    half_local = deconv_weight.shape[1]
    neck_local = lateral_coarse.shape[1]
    pixels = row_count * col_count
    coarse_pixels = row_count // 2 * (col_count // 2)
    deconv_flat = deconv_weight.reshape(4 * half_local, deconv_weight.shape[2])
    piece = lax.all_gather(features, "mp", axis=2, tiled=True)
    depth = piece.shape[2]
    flattened = piece.reshape(pixels, depth)
    raised = contract_last(deconv_flat, flattened)
    middle = contract_last(lateral_coarse[0], flattened)
    pooled_flat = pool_pairs(piece).reshape(coarse_pixels, depth)
    coarse = contract_last(lateral_coarse[1], pooled_flat)
    raised, middle, coarse = (raised, middle, coarse)
    raised = (
        raised.reshape(2, 2, half_local, row_count, col_count)
        + deconv_bias[None, None, :, None, None]
    )
    upsampled = raised.transpose(2, 3, 0, 4, 1).reshape(half_local, 4 * pixels).astype(jnp.bfloat16)
    piece = lax.all_gather(upsampled, "mp", axis=0, tiled=True)
    lateral_sum = jnp.dot(lateral_eight, piece, preferred_element_type=jnp.float32)
    lat_eight = lateral_sum.astype(jnp.bfloat16)
    lat_sixteen = middle.astype(jnp.bfloat16)
    lat_thirty = coarse.astype(jnp.bfloat16)
    level_eight = pyramid_level(
        lat_eight, 2 * row_count, 2 * col_count, 0, output_conv, norm_gain, norm_shift
    )
    level_sixteen = pyramid_level(
        lat_sixteen, row_count, col_count, 1, output_conv, norm_gain, norm_shift
    )
    level_thirty = pyramid_level(
        lat_thirty, row_count // 2, col_count // 2, 2, output_conv, norm_gain, norm_shift
    )
    level_sixty = level_thirty.reshape(neck_local, row_count // 2, col_count // 2)[
        :, ::2, ::2
    ].reshape(neck_local, -1)
    return (level_eight, level_sixteen, level_thirty, level_sixty)


def per_device(
    features,
    deconv_weight,
    deconv_bias,
    lateral_eight,
    lateral_coarse,
    output_conv,
    norm_gain,
    norm_shift,
):
    return channel_pyramid(
        features,
        deconv_weight,
        deconv_bias,
        lateral_eight,
        lateral_coarse,
        output_conv,
        norm_gain,
        norm_shift,
    )


def solution(mesh):
    return jax.shard_map(
        per_device,
        mesh=mesh,
        in_specs=(
            P(("dp", "space"), None, "mp"),
            P(None, "mp", None),
            P("mp"),
            P("mp", None),
            P(None, "mp", None),
            P(None, "mp", None, None),
            P(),
            P(),
        ),
        out_specs=(
            P("mp", ("dp", "space")),
            P("mp", ("dp", "space")),
            P("mp", ("dp", "space")),
            P("mp", ("dp", "space")),
        ),
        check_vma=False,
    )
```

profile of v0, /device:TPU:0, one launch (start us, length us, event | category | flops | bytes accessed | tf_op | source)
XLA Modules:
  0.0 179.7 jit_solution(12206708031647192003)
XLA Ops:
  7.2 0.7 all-gather.4.cloned.1.call-update
  8.0 0.9 fusion.99
  8.9 0.9 fusion.100
  9.8 0.7 fusion.86
  10.5 0.6 fusion.83
  11.1 0.7 fusion.82
  11.7 2.0 %slice_bitcast_fusion = (bf16[64,9,256]{2,0,1:T(8,128)(2,1)S(1)}, bf16[64,9,256]{2,0,1:T(8,128)(2,1)}, bf16[64,9,256]{2,0,1:T(8,128)(2,1)}) fusion(bf16[3,64,9,256]{3,1,2,0:T(8,128)(2,1)} %param.13), kind=kLoop, calls=%fused_computation.94 | loop fusion | bytes 1769472 | tf_op jit(solution)/shard_map/squeeze | solution.py:63
  13.8 25.2 %all-gather.4.cloned.1.call-done = bf16[8,64,1024]{2,1,0:T(8,128)(2,1)} async-done(((bf16[8,64,256]{2,1,0:T(8,128)(2,1)}), bf16[8,64,1024]{2,1,0:T(8,128)(2,1)}) %all-gather.4.cloned.1.call-update) | async-done | bytes 1048592 | tf_op jit(solution)/shard_map/all_gather | solution.py:96
  39.0 1.6 reshape.228
  40.5 2.5 %reduce_max.9 = bf16[4,32,1024]{2,1,0:T(8,128)(2,1)} reduce(bf16[4,2,32,2,1024]{4,3,2,1,0:T(2,128)(2,1)S(1)} %reshape.228, bf16[]{:T(256)} %constant.41.clone.1), dimensions={1,3}, to_apply=%region_12.13 | reduce | flops 393216 | bytes 1310722 | tf_op jit(solution)/shard_map/reduce_max | solution.py:24
  43.1 1.2 fusion.26
  44.3 8.2 %all_gather.19 = bf16[256,128]{1,0:T(8,128)(2,1)S(1)} all-gather(bf16[64,128]{1,0:T(8,128)(2,1)S(1)} %fusion.26), channel_id=1, replica_groups=mesh['dp'=4,'space'=2,'mp'=4] {'mp'}, dimensions={0}, use_global_device_ids=true | all-gather | bytes 81920 | tf_op jit(solution)/shard_map/all_gather | solution.py:65
  52.8 1.3 collective-permute-start.4
  54.1 1.3 collective-permute-start.5
  55.4 1.3 convolution_convert_fusion.1
  56.8 8.3 %all_gather.18 = bf16[256,512]{1,0:T(8,128)(2,1)S(1)} all-gather(bf16[64,512]{1,0:T(8,128)(2,1)S(1)} %convolution_convert_fusion.1), channel_id=1, replica_groups=mesh['dp'=4,'space'=2,'mp'=4] {'mp'}, dimensions={0}, use_global_device_ids=true | all-gather | bytes 327680 | tf_op jit(solution)/shard_map/all_gather | solution.py:65
  65.5 0.6 fusion.96
  66.1 1.4 collective-permute-start.2
  67.6 1.3 collective-permute-start.3
  68.9 0.7 fusion.15
  69.7 1.3 copy.13
  72.5 0.7 fusion.92
  73.7 33.4 %all-gather.6.cloned.1.call-done = bf16[512,2048]{0,1:T(8,128)(2,1)} async-done(((bf16[128,2048]{0,1:T(8,128)(2,1)}), bf16[512,2048]{0,1:T(8,128)(2,1)}) %all-gather.6.cloned.1.call-update) | async-done | bytes 2097168 | tf_op jit(solution)/shard_map/all_gather | solution.py:109
  107.1 3.0 %fusion.8 = bf16[64,2048]{1,0:T(8,128)(2,1)} fusion(bf16[512,2048]{0,1:T(8,128)(2,1)} %all-gather.6.cloned.1.call-done, bf16[64,512]{1,0:T(8,128)(2,1)S(1)} %copy-done.5), kind=kOutput, calls=%fused_computation.22 | convolution fusion | flops 134348800 | bytes 2424832 | tf_op jit(solution)/shard_map/dot_general | solution.py:110
  111.7 25.2 %all-gather.8.cloned.1.call-done = bf16[256,2048]{1,0:T(8,128)(2,1)} async-done(((bf16[64,2048]{1,0:T(8,128)(2,1)}), bf16[256,2048]{1,0:T(8,128)(2,1)}) %all-gather.8.cloned.1.call-update) | async-done | bytes 1048592 | tf_op jit(solution)/shard_map/all_gather | solution.py:65
  136.8 1.5 convert_reduce_fusion
  138.4 1.7 fusion.89
  140.5 1.6 collective-permute-start
  142.1 1.5 collective-permute-start.1
  143.6 0.2 fusion.91
  143.8 1.5 collective-permute-done.1
  145.4 2.9 %fusion.5 = bf16[256,18,130]{2,1,0:T(8,128)(2,1)S(1)} fusion(bf16[256,1,128]{2,1,0:T(2,128)(2,1)S(1)} %collective-permute-done.1, bf16[256,16,128]{2,1,0:T(8,128)(2,1)S(1)} %bitcast.224, bf16[256,1,128]{2,1,0:T(2,128)(2,1)S(1)} %collective-permute-done), kind=kLoop, calls=%fused_computation.7 | loop fusion | flops 7188480 | bytes 2377728 | tf_op jit(solution)/shard_map/concatenate | solution.py:18
  148.3 2.2 %fusion.93 = (bf16[256,16,128]{2,1,0:T(8,128)(2,1)S(1)}, bf16[256,16,128]{2,1,0:T(8,128)(2,1)S(1)}, bf16[256,16,128]{2,1,0:T(8,128)(2,1)S(1)}, bf16[256,16,128]{...) fusion(bf16[256,18,130]{2,1,0:T(8,128)(2,1)S(1)} %fusion.5), kind=kLoop, calls=%fused_computation.189 | loop fusion | bytes 12582912 | tf_op jit(solution)/shard_map/slice | solution.py:51
  150.5 0.3 fusion.41
  150.8 1.1 pad_maximum_fusion
  151.9 0.3 convolution_add_fusion.7
  152.2 0.3 convolution_add_fusion.6
  152.5 0.3 convolution_add_fusion.5
  152.8 0.6 copy-done.1
  153.4 0.6 convolution_add_fusion.4
  154.0 0.3 convolution_add_fusion.3
  154.3 0.3 convolution_add_fusion.2
  154.7 0.3 convolution_add_fusion.1
  155.0 0.3 fusion.90
  155.3 15.3 %all-reduce.3 = (f32[2048]{0:T(1024)S(1)}, f32[2048]{0:T(1024)S(1)}, f32[512]{0:T(512)S(1)}, f32[512]{0:T(512)S(1)}, f32[128]{0:T(128)S(1)}, /*index=5*/f32[128]{0:T(128)S(1)}) all-reduce(f32[2048]{0:T(1024)S(1)} %get-tuple-element.7, f32[2048]{0:T(1024)S(1)} %get-tuple-element.6, ...), channel_id=1, replica_groups=mesh['dp'=4,'space'=2,'mp'=4] {'mp'}, use_global_device_ids=true, to_apply=%region_5.6 | all-reduce | flops 5376 | bytes 43008 | tf_op jit(solution)/shard_map/psum | solution.py:74
  170.9 0.7 slice.317
  171.6 0.7 fusion.72
  172.3 0.8 fusion.56
  (76 shorter events, 4.8 us)
Async XLA Ops:
  7.2 61.7 %copy-start = (bf16[4,128,1024]{2,1,0:T(8,128)(2,1)S(1)}, bf16[4,128,1024]{2,1,0:T(8,128)(2,1)}, u32[]{:S(2)}) copy-start(bf16[4,128,1024]{2,1,0:T(8,128)(2,1)} %param.9) | copy-start | bytes 3145732
  7.2 31.8 %all-gather.4.cloned.1.call-start = ((), (), s32[]{:S(2)}) async-start(), calls=%async_computation | async-start | bytes 1310720 | tf_op jit(solution)/shard_map/all_gather | solution.py:96
  7.9 99.2 %all-gather.6.cloned.1.call-start = ((), (), s32[]{:S(2)}) async-start(), calls=%async_computation.1 | async-start | bytes 2621440 | tf_op jit(solution)/shard_map/all_gather | solution.py:109
  39.0 16.5 %copy-start.2 = (bf16[8,64,1024]{2,1,0:T(8,128)(2,1)S(1)}, bf16[8,64,1024]{2,1,0:T(8,128)(2,1)}, u32[]{:S(2)}) copy-start(bf16[8,64,1024]{2,1,0:T(8,128)(2,1)} %all-gather.4.cloned.1.call-done) | copy-start | bytes 3145732
  43.1 25.9 %copy-start.13 = (f32[128]{0:T(128)S(1)}, f32[128]{0:T(128)}, u32[]{:S(2)}) copy-start(f32[128]{0:T(128)} %param.10) | copy-start | bytes 1540
  52.8 18.3 %collective-permute-start.4 = (bf16[256,1,32]{0,2,1:T(8,128)(2,1)S(1)}, bf16[256,1,32]{0,2,1:T(8,128)(2,1)S(1)}, u32[]{:S(2)}, u32[]{:S(2)}) collective-permute-start(bf16[256,1,32]{0,2,1:T(8,128)(2,1)S(1)} %get-tuple-element.53), channel_id=1, source_target_pairs={{0,4},{1,5},{2,6},{3,7},{8,12},{9,13},{10,14},{11,15},{16,20},{17,... | collective-permute-start | bytes 49160 | tf_op jit(solution)/shard_map/ppermute | solution.py:14
  54.1 17.0 %collective-permute-start.5 = (bf16[256,1,32]{0,2,1:T(8,128)(2,1)S(1)}, bf16[256,1,32]{0,2,1:T(8,128)(2,1)S(1)}, u32[]{:S(2)}, u32[]{:S(2)}) collective-permute-start(bf16[256,1,32]{0,2,1:T(8,128)(2,1)S(1)} %get-tuple-element.54), channel_id=1, source_target_pairs={{4,0},{5,1},{6,2},{7,3},{12,8},{13,9},{14,10},{15,11},{20,16},{21,... | collective-permute-start | bytes 49160 | tf_op jit(solution)/shard_map/ppermute | solution.py:17
  66.1 7.0 %collective-permute-start.2 = (bf16[256,1,64]{0,2,1:T(8,128)(2,1)}, bf16[256,1,64]{0,2,1:T(8,128)(2,1)S(1)}, u32[]{:S(2)}, u32[]{:S(2)}) collective-permute-start(bf16[256,1,64]{0,2,1:T(8,128)(2,1)} %get-tuple-element.43), channel_id=1, source_target_pairs={{0,4},{1,5},{2,6},{3,7},{8,12},{9,13},{10,14},{11,15},{16,20},{17,... | collective-permute-start | bytes 98312 | tf_op jit(solution)/shard_map/ppermute | solution.py:14
  67.6 5.6 %collective-permute-start.3 = (bf16[256,1,64]{0,2,1:T(8,128)(2,1)}, bf16[256,1,64]{0,2,1:T(8,128)(2,1)S(1)}, u32[]{:S(2)}, u32[]{:S(2)}) collective-permute-start(bf16[256,1,64]{0,2,1:T(8,128)(2,1)} %get-tuple-element.44), channel_id=1, source_target_pairs={{4,0},{5,1},{6,2},{7,3},{12,8},{13,9},{14,10},{15,11},{20,16},{21,... | collective-permute-start | bytes 98312 | tf_op jit(solution)/shard_map/ppermute | solution.py:17
  71.0 65.8 %all-gather.8.cloned.1.call-start = ((), (), s32[]{:S(2)}) async-start(), calls=%async_computation.2 | async-start | bytes 1310720 | tf_op jit(solution)/shard_map/all_gather | solution.py:65
  72.3 1.2 copy-start.3
  73.1 34.0 %copy-start.5 = (bf16[64,512]{1,0:T(8,128)(2,1)S(1)}, bf16[64,512]{1,0:T(8,128)(2,1)}, u32[]{:S(2)}) copy-start(bf16[64,512]{1,0:T(8,128)(2,1)} %param.11) | copy-start | bytes 196612
  140.5 3.3 %collective-permute-start = (bf16[256,1,128]{2,1,0:T(2,128)(2,1)S(1)}, bf16[256,1,128]{2,1,0:T(2,128)(2,1)S(1)}, u32[]{:S(2)}, u32[]{:S(2)}) collective-permute-start(bf16[256,1,128]{2,1,0:T(2,128)(2,1)S(1)} %get-tuple-element.30), channel_id=1, source_target_pairs={{0,4},{1,5},{2,6},{3,7},{8,12},{9,13},{10,14},{11,15},{16,20},{17,... | collective-permute-start | bytes 196616 | tf_op jit(solution)/shard_map/ppermute | solution.py:14
  142.1 3.2 %collective-permute-start.1 = (bf16[256,1,128]{2,1,0:T(2,128)(2,1)S(1)}, bf16[256,1,128]{2,1,0:T(2,128)(2,1)S(1)}, u32[]{:S(2)}, u32[]{:S(2)}) collective-permute-start(bf16[256,1,128]{2,1,0:T(2,128)(2,1)S(1)} %get-tuple-element.31), channel_id=1, source_target_pairs={{4,0},{5,1},{6,2},{7,3},{12,8},{13,9},{14,10},{15,11},{20,16},{21,... | collective-permute-start | bytes 196616 | tf_op jit(solution)/shard_map/ppermute | solution.py:17
  148.3 2.2 %copy-start.4 = (bf16[64,9,256]{2,0,1:T(8,128)(2,1)S(1)}, bf16[64,9,256]{2,0,1:T(8,128)(2,1)}, u32[]{:S(2)}) copy-start(bf16[64,9,256]{2,0,1:T(8,128)(2,1)} %get-tuple-element.33) | copy-start | bytes 884740
  152.2 1.2 copy-start.1
  154.6 0.7 copy-start.11
  154.6 0.7 copy-start.12
  154.6 16.0 %copy-start.9 = (f32[64]{0:T(128)S(1)}, f32[64]{0:T(128)}, u32[]{:S(2)}) copy-start(f32[64]{0:T(128)} %get-tuple-element.86) | copy-start | bytes 772
  154.7 16.0 %copy-start.10 = (f32[64]{0:T(128)S(1)}, f32[64]{0:T(128)}, u32[]{:S(2)}) copy-start(f32[64]{0:T(128)} %get-tuple-element.87) | copy-start | bytes 772
  154.7 16.9 %copy-start.7 = (f32[64]{0:T(128)S(1)}, f32[64]{0:T(128)}, u32[]{:S(2)}) copy-start(f32[64]{0:T(128)} %get-tuple-element.83) | copy-start | bytes 772
  154.7 16.9 %copy-start.8 = (f32[64]{0:T(128)S(1)}, f32[64]{0:T(128)}, u32[]{:S(2)}) copy-start(f32[64]{0:T(128)} %get-tuple-element.85) | copy-start | bytes 772
  170.8 2.4 %copy-start.6 = (bf16[64,128]{1,0:T(8,128)(2,1)}, bf16[64,128]{1,0:T(8,128)(2,1)S(1)}, u32[]{:S(2)}) copy-start(bf16[64,128]{1,0:T(8,128)(2,1)S(1)} %fusion.81) | copy-start | bytes 49156
Sparse Core Ops, SparseCore 0:
  9.8 29.1 all-gather.3
  71.2 35.9 all-gather.5
  110.3 26.4 all-gather.7
where the time goes:
time: 180 us
  waiting for transfers between devices  86.1 us (48%)
  blocking collectives  31.9 us (18%)
  between operations  14.3 us (8%)
  local copies, waits for them, and re-layouts  13.9 us (8%)
  matrix products  13 us (7%)
  other arithmetic  12.1 us (7%)
  starting transfers between devices  8.49 us (5%)
    all_gather x1, waiting for transfers between devices, channel_pyramid(): piece = lax.all_gather(upsampled, 'mp', axis=0, tiled=True)  33.4 us
    all_gather x1, waiting for transfers between devices, channel_pyramid(): piece = lax.all_gather(features, 'mp', axis=2, tiled=True)  25.2 us
    all_gather x1, waiting for transfers between devices, pyramid_level(): gathered = lax.all_gather(lateral, 'mp', axis=0, tiled=True)  25.2 us
    all_gather x2, blocking collectives, pyramid_level(): gathered = lax.all_gather(lateral, 'mp', axis=0, tiled=True)  16.6 us
    psum x1, blocking collectives, pyramid_level(): sums, squares = lax.psum(cell_moments(convolved), 'mp')  15.3 us
    dot_general x27, matrix products, conv_taps(): jnp.dot(rows_used, window, preferred_element_type=jnp.float32)  6.68 us
    ppermute x3, starting transfers between devices, extended(): lax.ppermute(lax.slice_in_dim(block, block.shape[dim] - width, None, axis...  4.31 us
    concatenate x6, other arithmetic, extended(): block = jnp.concatenate([low, block, high], axis=dim)  4.2 us
  transfers between devices with their start and end apart: 9, of which 4 were waited for; matrix products, arithmetic and copies ran while one was open for 8% of the time, Pallas kernels for 0%

commit v1 on v0

--- a/solution.py
+++ b/solution.py
@@ -1,9 +1,14 @@
+import functools
+
 import jax
 import jax.numpy as jnp
 from jax import lax
+from jax.experimental import pallas as pl
+from jax.experimental.pallas import tpu as pltpu
 from jax.sharding import PartitionSpec as P
 
 EPSILON = 1e-06
+MESH = pl.DeviceIdType.MESH
 
 
 def extended(block, sides, width):
@@ -126,26 +131,380 @@
     return (level_eight, level_sixteen, level_thirty, level_sixty)
 
 
-def per_device(
-    features,
-    deconv_weight,
-    deconv_bias,
-    lateral_eight,
-    lateral_coarse,
-    output_conv,
-    norm_gain,
-    norm_shift,
+def nt(left, right):
+    return lax.dot_general(
+        left, right, (((1,), (1,)), ((), ())), preferred_element_type=jnp.float32
+    )
+
+
+def lane_norm(values, gain_row, shift_row):
+    floats = values.astype(jnp.float32)
+    center = jnp.mean(floats, axis=1, keepdims=True)
+    spread = jnp.mean(floats * floats, axis=1, keepdims=True) - center * center
+    scaled = (floats - center) * lax.rsqrt(spread + EPSILON)
+    return scaled * gain_row + shift_row
+
+
+def shifted(values, step, cols):
+    count = values.shape[0]
+    moved = pltpu.roll(values, step % count, 0)
+    col = lax.rem(lax.broadcasted_iota(jnp.int32, values.shape, 0), cols)
+    edge = 0 if step > 0 else cols - 1
+    return jnp.where(col == edge, 0.0, moved)
+
+
+FEAT, LATW, CONVW, RAISE, COARSE, MOMENT, FINAL = range(7)
+KINDS = 7
+
+
+def pyramid_kernel(
+    n, bands, rows, cols, neck, half,
+    feat, dw, bias, lat, lc, oc, gain, shift, gcol, scol,
+    o8, o16, o32, o64,
+    fbuf, dwv, lcv, latw, w0, w1, w2, acc, pool, ubuf, usend, cbuf, v8, x16, x32,
+    halo8, halo16, halo32, send8, send16, send32, mbuf, inter, osend,
+    ssem, rsem, lsem, hs, hr,
 ):
-    return channel_pyramid(
-        features,
-        deconv_weight,
-        deconv_bias,
-        lateral_eight,
-        lateral_coarse,
-        output_conv,
-        norm_gain,
-        norm_shift,
-    )
+    me = lax.axis_index("mp")
+    band = lax.axis_index("space")
+    depth = feat.shape[1]
+    own = neck // n
+    hown = half // n
+    px = rows * cols
+    prows = rows // n
+    part = prows * cols
+    nine = 9 * neck
+    r2, c2 = rows // 2, cols // 2
+    px2 = r2 * c2
+
+    def at_mp(k):
+        return lax.rem(me + k, n)
+
+    locals_ = [
+        pltpu.make_async_copy(feat, fbuf.at[0], lsem.at[0]),
+        pltpu.make_async_copy(dw, dwv, lsem.at[1]),
+        pltpu.make_async_copy(lc, lcv, lsem.at[2]),
+        pltpu.make_async_copy(lat, latw.at[pl.ds(pl.multiple_of(me * own, own), own)], lsem.at[3]),
+        pltpu.make_async_copy(oc.at[0], w0.at[pl.ds(pl.multiple_of(me * own, own), own)], lsem.at[4]),
+        pltpu.make_async_copy(oc.at[1], w1, lsem.at[5]),
+        pltpu.make_async_copy(oc.at[2], w2, lsem.at[6]),
+    ]
+    for copy in locals_:
+        copy.start()
+
+    barrier = pltpu.get_barrier_semaphore()
+    for b in range(bands):
+        for k in range(n):
+            if b == 0 and k == 0:
+                continue
+            pl.semaphore_signal(
+                barrier,
+                inc=1,
+                device_id={"space": lax.rem(band + b, bands), "mp": at_mp(k)},
+                device_id_type=MESH,
+            )
+    pl.semaphore_wait(barrier, bands * n - 1)
+
+    def remote(src, dst, kind, k):
+        return pltpu.make_async_remote_copy(
+            src_ref=src,
+            dst_ref=dst,
+            send_sem=ssem.at[kind, k],
+            recv_sem=rsem.at[kind, k],
+            device_id={"mp": at_mp(k)},
+            device_id_type=MESH,
+        )
+
+    peers = list(range(1, n))
+    mine = pl.ds(pl.multiple_of(me * own, own), own)
+    sends = {}
+
+    def launch(kind, make):
+        for k in peers:
+            copy = remote(*make(k), kind, k)
+            copy.start()
+            sends[kind, k] = copy
+
+    launch(FEAT, lambda k: (feat, fbuf.at[k]))
+    launch(LATW, lambda k: (lat, latw.at[mine]))
+
+    lat16 = jnp.zeros((own, px), jnp.float32)
+    lat32 = jnp.zeros((own, px2), jnp.float32)
+    for k in range(n):
+        if k == 0:
+            for i in range(3):
+                locals_[i].wait()
+        else:
+            sends[FEAT, k].wait_recv()
+        src = lax.rem(me - k + n, n)
+        span = pl.ds(pl.multiple_of(src * depth, depth), depth)
+        block = fbuf[k]
+        term = nt(block, dwv[:, span])
+        if k == 0:
+            acc[...] = term
+        else:
+            acc[...] += term
+        lat16 = lat16 + nt(lcv[0:own, span], block)
+        floats = block.astype(jnp.float32).reshape(r2, 2 * cols, depth)
+        tall = jnp.maximum(floats[:, :cols], floats[:, cols:]).reshape(r2 * cols, depth)
+        halves = []
+        for g in range(depth // 128):
+            pool[...] = tall[:, g * 128 : (g + 1) * 128]
+            halves.append(jnp.maximum(pool[pl.ds(0, px2, stride=2), :], pool[pl.ds(1, px2, stride=2), :]))
+        pooled = jnp.concatenate(halves, axis=1).astype(jnp.bfloat16)
+        lat32 = lat32 + nt(lcv[own:, span], pooled)
+
+    for d in range(n):
+        for il in range(prows):
+            base = (d * prows + il) * cols
+            for a in range(2):
+                for b in range(2):
+                    tap = 2 * a + b
+                    value = acc[base : base + cols, tap * hown : (tap + 1) * hown] + bias[...]
+                    at = (b * 2 * prows + 2 * il + a) * cols
+                    usend[d, at : at + cols, :] = value.astype(jnp.bfloat16)
+    launch(RAISE, lambda k: (usend.at[at_mp(k)], ubuf.at[k]))
+    cbuf[mine, 0:px] = lat16.astype(jnp.bfloat16)
+    cbuf[mine, px:] = lat32.astype(jnp.bfloat16)
+    launch(COARSE, lambda k: (cbuf.at[mine], cbuf.at[mine]))
+    locals_[4].wait()
+    launch(CONVW, lambda k: (oc.at[0], w0.at[mine]))
+
+    locals_[3].wait()
+    for k in peers:
+        sends[LATW, k].wait_recv()
+    total = nt(usend[me], latw[:, pl.ds(pl.multiple_of(me * hown, hown), hown)])
+    for k in peers:
+        sends[RAISE, k].wait_recv()
+        src = lax.rem(me - k + n, n)
+        total = total + nt(ubuf[k], latw[:, pl.ds(pl.multiple_of(src * hown, hown), hown)])
+    own_rows = 2 * prows
+    wide = own_rows * cols
+    normed = lane_norm(total.astype(jnp.bfloat16), gain[0:1, :], shift[0:1, :])
+    rounded = normed.astype(jnp.bfloat16)
+    for b in range(2):
+        send8[0, b * cols : (b + 1) * cols, :] = rounded[b * wide : b * wide + cols]
+        send8[1, b * cols : (b + 1) * cols, :] = rounded[(b + 1) * wide - cols : (b + 1) * wide]
+
+    place = band * n + me
+    last = bands * n - 1
+
+    def halo(src_buf, dst_buf, level, low_if, low_dev, high_if, high_dev):
+        low = pltpu.make_async_remote_copy(
+            src_ref=src_buf.at[0], dst_ref=dst_buf.at[1], send_sem=hs.at[level, 0],
+            recv_sem=hr.at[level, 1], device_id=low_dev, device_id_type=MESH)
+        high = pltpu.make_async_remote_copy(
+            src_ref=src_buf.at[1], dst_ref=dst_buf.at[0], send_sem=hs.at[level, 1],
+            recv_sem=hr.at[level, 0], device_id=high_dev, device_id_type=MESH)
+
+        @pl.when(low_if)
+        def _():
+            low.start()
+
+        @pl.when(high_if)
+        def _():
+            high.start()
+
+        def finish():
+            @pl.when(low_if)
+            def _():
+                low.wait_send()
+                high_like = pltpu.make_async_remote_copy(
+                    src_ref=src_buf.at[1], dst_ref=dst_buf.at[0], send_sem=hs.at[level, 1],
+                    recv_sem=hr.at[level, 0], device_id=low_dev, device_id_type=MESH)
+                high_like.wait_recv()
+
+            @pl.when(high_if)
+            def _():
+                high.wait_send()
+                low_like = pltpu.make_async_remote_copy(
+                    src_ref=src_buf.at[0], dst_ref=dst_buf.at[1], send_sem=hs.at[level, 0],
+                    recv_sem=hr.at[level, 1], device_id=high_dev, device_id_type=MESH)
+                low_like.wait_recv()
+
+            @pl.when(jnp.logical_not(low_if))
+            def _():
+                dst_buf[0] = jnp.zeros(dst_buf.shape[1:], dst_buf.dtype)
+
+            @pl.when(jnp.logical_not(high_if))
+            def _():
+                dst_buf[1] = jnp.zeros(dst_buf.shape[1:], dst_buf.dtype)
+
+        return finish
+
+    def device_of(index):
+        return {"space": lax.div(index, n), "mp": lax.rem(index, n)}
+
+    finish8 = halo(
+        send8, halo8, 0,
+        place > 0, device_of(jnp.maximum(place - 1, 0)),
+        place < last, device_of(jnp.minimum(place + 1, last)),
+    )
+    zero = normed[0:wide]
+    one = normed[wide:]
+
+    def fill8(at, count, even, odd):
+        v8[0, at : at + count, :] = shifted(odd, 1, cols).astype(jnp.bfloat16)
+        v8[1, at : at + count, :] = even.astype(jnp.bfloat16)
+        v8[2, at : at + count, :] = odd.astype(jnp.bfloat16)
+        v8[3, at : at + count, :] = shifted(even, -1, cols).astype(jnp.bfloat16)
+
+    fill8(cols, wide, zero, one)
+
+    for k in peers:
+        sends[COARSE, k].wait_recv()
+    coarse = cbuf[...].astype(jnp.float32).T
+    levels = (
+        (1, rows, cols, x16, send16, halo16, w1, coarse[:px], 0),
+        (2, r2, c2, x32, send32, halo32, w2, coarse[px:], px),
+    )
+
+    def fill(x, at, count, values, width):
+        x[0, at : at + count, :] = shifted(values, 1, width).astype(jnp.bfloat16)
+        x[1, at : at + count, :] = values.astype(jnp.bfloat16)
+        x[2, at : at + count, :] = shifted(values, -1, width).astype(jnp.bfloat16)
+
+    finishes = []
+    for level, height, width, x, snd, hal, w, values, at in levels:
+        out = lane_norm(values, gain[2 * level : 2 * level + 1, :], shift[2 * level : 2 * level + 1, :])
+        fill(x, width, height * width, out, width)
+        snd[0] = out[:width].astype(jnp.bfloat16)
+        snd[1] = out[height * width - width :].astype(jnp.bfloat16)
+        finishes.append(halo(
+            snd, hal, level,
+            band > 0, {"space": jnp.maximum(band - 1, 0)},
+            band < bands - 1, {"space": jnp.minimum(band + 1, bands - 1)},
+        ))
+    maps = []
+    locals_[5].wait()
+    locals_[6].wait()
+    for (level, height, width, x, snd, hal, w, values, at), done in zip(levels, finishes):
+        done()
+        fill(x, 0, width, hal[0].astype(jnp.float32), width)
+        fill(x, (height + 1) * width, width, hal[1].astype(jnp.float32), width)
+        result = jnp.zeros((own, height * width), jnp.float32)
+        for tap in range(9):
+            r, q = tap // 3, tap % 3
+            result = result + nt(
+                w[:, tap * neck : (tap + 1) * neck], x[q, r * width : (r + height) * width, :]
+            )
+        result = result.astype(jnp.bfloat16).astype(jnp.float32)
+        span = slice(at, at + height * width)
+        mbuf[0, 0:1, span] = jnp.sum(result, axis=0, keepdims=True)
+        mbuf[0, 1:2, span] = jnp.sum(result * result, axis=0, keepdims=True)
+        maps.append(result)
+    launch(MOMENT, lambda k: (mbuf.at[0], mbuf.at[k]))
+
+    finish8()
+    fill8(0, cols, halo8[0, 0:cols].astype(jnp.float32), halo8[0, cols:].astype(jnp.float32))
+    fill8(cols + wide, cols, halo8[1, 0:cols].astype(jnp.float32), halo8[1, cols:].astype(jnp.float32))
+    for k in peers:
+        sends[CONVW, k].wait_recv()
+    for b in range(2):
+        result = jnp.zeros((wide, neck), jnp.float32)
+        for tap in range(9):
+            r, q = tap // 3, tap % 3
+            result = result + nt(
+                v8[b + q, r * cols : r * cols + wide, :], w0[:, tap * neck : (tap + 1) * neck]
+            )
+        out = lane_norm(result.astype(jnp.bfloat16), gain[1:2, :], shift[1:2, :])
+        for g in range(neck // 128):
+            inter[g, pl.ds(b, wide, stride=2), :] = out[:, g * 128 : (g + 1) * 128]
+    for g in range(neck // 128):
+        osend[g * 128 : (g + 1) * 128, :] = inter[g].T.astype(jnp.bfloat16)
+    cells = pl.ds(pl.multiple_of(me * 2 * wide, 2 * wide), 2 * wide)
+    launch(FINAL, lambda k: (osend.at[pl.ds(pl.multiple_of(at_mp(k) * own, own), own)], o8.at[:, cells]))
+    o8[:, cells] = osend[mine, :]
+
+    for k in peers:
+        sends[MOMENT, k].wait_recv()
+    moments = mbuf[0]
+    for k in peers:
+        moments = moments + mbuf[k]
+    moments = moments / neck
+    for (level, height, width, x, snd, hal, w, values, at), result in zip(levels, maps):
+        span = slice(at, at + height * width)
+        center = moments[0:1, span]
+        spread = moments[1:2, span] - center * center
+        scaled = (result - center) * lax.rsqrt(spread + EPSILON)
+        final = (scaled * gcol[:, level : level + 1] + scol[:, level : level + 1]).astype(jnp.bfloat16)
+        if level == 1:
+            o16[...] = final
+        else:
+            o32[...] = final
+            count = o64.shape[1]
+            wide2 = c2 // 2
+            cell = lax.broadcasted_iota(jnp.int32, (px2, count), 0)
+            target = lax.broadcasted_iota(jnp.int32, (px2, count), 1)
+            wanted = lax.div(target, wide2) * (2 * c2) + 2 * lax.rem(target, wide2)
+            pick = jnp.where(cell == wanted, 1.0, 0.0).astype(jnp.bfloat16)
+            o64[...] = jnp.dot(final, pick, preferred_element_type=jnp.float32).astype(jnp.bfloat16)
+
+    for kind in range(KINDS):
+        for k in peers:
+            sends[kind, k].wait_send()
+    for k in peers:
+        sends[FINAL, k].wait_recv()
+
+
+def fused(features, deconv_weight, deconv_bias, lateral_eight, lateral_coarse, output_conv,
+          norm_gain, norm_shift):
+    n = lax.axis_size("mp")
+    bands = lax.axis_size("space")
+    rows, cols, depth = features.shape
+    full = deconv_weight.shape[2]
+    hown = deconv_weight.shape[1]
+    own = lateral_eight.shape[0]
+    neck, half = own * n, hown * n
+    px, px2 = rows * cols, rows * cols // 4
+    wide = 2 * (rows // n) * cols
+    first = lax.axis_index("mp") * own
+    gcol = lax.dynamic_slice_in_dim(norm_gain[1::2], first, own, 1).T
+    scol = lax.dynamic_slice_in_dim(norm_shift[1::2], first, own, 1).T
+    bf, f32 = jnp.bfloat16, jnp.float32
+    vmem = pl.BlockSpec(memory_space=pltpu.VMEM)
+    hbm = pl.BlockSpec(memory_space=pl.ANY)
+    shapes = [
+        ((n, px, depth), bf), ((4 * hown, full), bf), ((2 * own, full), bf),
+        ((neck, half), bf), ((neck, 9 * neck), bf), ((own, 9 * neck), bf), ((own, 9 * neck), bf),
+        ((px, 4 * hown), f32), ((px // 2, 128), f32), ((n, 2 * wide, hown), bf),
+        ((n, 2 * wide, hown), bf), ((neck, px + px2), bf),
+        ((4, wide + 2 * cols, neck), bf), ((3, px + 2 * cols, neck), bf),
+        ((3, px2 + cols, neck), bf),
+        ((2, 2 * cols, neck), bf), ((2, cols, neck), bf), ((2, cols // 2, neck), bf),
+        ((2, 2 * cols, neck), bf), ((2, cols, neck), bf), ((2, cols // 2, neck), bf),
+        ((n, 8, px + px2), f32), ((neck // 128, 2 * wide, 128), f32), ((neck, 2 * wide), bf),
+    ]
+    return pl.pallas_call(
+        functools.partial(pyramid_kernel, n, bands, rows, cols, neck, half),
+        out_shape=[
+            jax.ShapeDtypeStruct((own, 4 * px), bf), jax.ShapeDtypeStruct((own, px), bf),
+            jax.ShapeDtypeStruct((own, px2), bf), jax.ShapeDtypeStruct((own, px2 // 4), bf),
+        ],
+        in_specs=[hbm, hbm, vmem, hbm, hbm, hbm, vmem, vmem, vmem, vmem],
+        out_specs=[vmem] * 4,
+        scratch_shapes=[pltpu.VMEM(s, d) for s, d in shapes] + [
+            pltpu.SemaphoreType.DMA((KINDS, n)), pltpu.SemaphoreType.DMA((KINDS, n)),
+            pltpu.SemaphoreType.DMA((7,)), pltpu.SemaphoreType.DMA((3, 2)),
+            pltpu.SemaphoreType.DMA((3, 2)),
+        ],
+        compiler_params=pltpu.CompilerParams(
+            collective_id=0, has_side_effects=True, vmem_limit_bytes=56 << 20
+        ),
+    )(
+        features.reshape(px, depth), deconv_weight.reshape(4 * hown, full),
+        deconv_bias.reshape(1, hown), lateral_eight, lateral_coarse.reshape(2 * own, full),
+        output_conv.reshape(3, own, 9 * neck), norm_gain, norm_shift, gcol, scol,
+    )
+
+
+def per_device(features, deconv_weight, *rest):
+    n = lax.axis_size("mp")
+    rows, cols, depth = features.shape
+    aligned = depth % 128 == 0 and deconv_weight.shape[1] % 128 == 0
+    if aligned and rows % n == 0 and rows % 4 == 0 and cols % 64 == 0:
+        return tuple(fused(features, deconv_weight, *rest))
+    return channel_pyramid(features, deconv_weight, *rest)
 
 
 def solution(mesh):

time: 180 us -> 62.5 us (0.35)
  waiting for transfers between devices: 86.1 us -> 0 us
  Pallas kernels: 0 us -> 52.6 us
  blocking collectives: 31.9 us -> 0 us
  between operations: 14.3 us -> 0.67 us
  matrix products: 13 us -> 0 us
  other arithmetic: 12.1 us -> 0 us
  starting transfers between devices: 8.49 us -> 0 us
  local copies, waits for them, and re-layouts: 13.9 us -> 8.78 us
    all_gather x3 -> x0, waiting for transfers between devices: 83.8 us -> none  [the longest x1 33.4 us: channel_pyramid(): piece = lax.all_gather(upsampled, 'mp', axis=0, tiled=True)]
    pallas_call x0 -> x1, Pallas kernels: none -> 52.6 us  [fused(): pl.pallas_call(functools.partial(pyramid_kernel, n, bands, rows, cols, ne...]
    all_gather x2 -> x0, blocking collectives: 16.6 us -> none  [pyramid_level(): gathered = lax.all_gather(lateral, 'mp', axis=0, tiled=True)]
    psum x1 -> x0, blocking collectives: 15.3 us -> none  [pyramid_level(): sums, squares = lax.psum(cell_moments(convolved), 'mp')]
    dot_general x31 -> x0, matrix products: 13 us -> none  [the longest x27 6.68 us: conv_taps(): jnp.dot(rows_used, window, preferred_element_type=jnp.float32)]
    ppermute x6 -> x0, starting transfers between devices: 8.37 us -> none  [the longest x3 4.31 us: extended(): lax.ppermute(lax.slice_in_dim(block, block.shape[dim] - width, None, axis...]
    slice x9 -> x2, local copies, waits for them, and re-layouts: 5.79 us -> 0.04 us  [the longest x1 0.02 us: fused(): scol = lax.dynamic_slice_in_dim(norm_shift[1::2], first, own, 1).T]
    unnamed x29 -> x13, local copies, waits for them, and re-layouts: 0.9 us -> 5.13 us
  transfers between devices with their start and end apart: 9 -> 0, of which waited for: 4 -> 0; matrix products, arithmetic and copies ran while one was open for 8% -> 0% of each run, Pallas kernels for 0% -> 0%
where the time goes in v1:
time: 62.5 us; the launch traced here: 62 us
  Pallas kernels  52.6 us (84%)
  local copies, waits for them, and re-layouts  8.78 us (14%)
  between operations  0.67 us (1%)
    pallas_call x1, Pallas kernels, fused(): pl.pallas_call(functools.partial(pyramid_kernel, n, bands, rows, cols, ne...  52.6 us
    unnamed x13, local copies, waits for them, and re-layouts  5.13 us
    reshape x1, local copies, waits for them, and re-layouts, fused(): output_conv.reshape(3, own, 9 * neck)  2.14 us
    pallas_call x1, local copies, waits for them, and re-layouts, fused(): pl.pallas_call(functools.partial(pyramid_kernel, n, bands, rows, cols, ne...  1.39 us

profile of v1, /device:TPU:0, one launch (start us, length us, event | category | flops | bytes accessed | tf_op | source)
XLA Modules:
  0.0 62.0 jit_solution(3767334771012988333)
XLA Ops:
  0.6 0.0 copy-start.1
  0.6 0.0 copy-start.2
  0.7 0.7 %copy-done.1 = f32[6,256]{1,0:T(8,128)S(1)} copy-done((f32[6,256]{1,0:T(8,128)S(1)}, f32[6,256]{1,0:T(8,128)}, u32[]{:S(2)}) %copy-start.1) | copy-done | bytes 6168
  1.4 0.0 copy-done.2
  1.4 0.1 constant_dynamic-slice_fusion
  1.4 0.7 %copy.21 = f32[3,64]{0,1:T(8,128)} copy(f32[3,64]{1,0:T(4,128)S(1)} %get-tuple-element.12) | data formatting | bytes 1536
  2.2 0.7 %copy.20 = f32[3,64]{0,1:T(8,128)} copy(f32[3,64]{1,0:T(4,128)S(1)} %get-tuple-element.13) | data formatting | bytes 1536
  2.9 2.1 %copy.22 = bf16[3,9,8,8,256]{4,3,1,2,0:T(8,128)(2,1)} copy(bf16[3,9,8,8,256]{4,3,2,1,0:T(8,128)(2,1)} %bitcast.10) | data formatting | bytes 1769472 | tf_op jit(solution)/shard_map/reshape | solution.py:497
  5.0 52.6 %shard_map.111 = (bf16[64,2048]{1,0:T(8,128)(2,1)}, bf16[64,512]{1,0:T(8,128)(2,1)}, bf16[64,128]{1,0:T(8,128)(2,1)}, bf16[64,32]{1,0:T(8,128)(2,1)}) custom-call(bf16[512,256]{1,0:T(8,128)(2,1)} %bitcast.11, bf16[512,1024]{1,0:T(8,128)(2,1)} %bitcast.9, f32[1,128]{1,0:T(1,128)} %bitcast.15, bf16[64,512]{1,0:T(8,128)(2,1)} %lat.1, ...), custom_call_target="tpu_custom_call" | custom-call | tf_op jit(solution)/shard_map/pallas_call | solution.py:478
  57.6 1.4 %copy.19 = bf16[64,32]{0,1:T(8,128)(2,1)} copy(bf16[64,32]{1,0:T(8,128)(2,1)} %get-tuple-element.11) | data formatting | bytes 8192 | tf_op jit(solution)/shard_map/pallas_call | solution.py:478
  59.0 0.0 copy-start
  59.0 1.7 %copy.26 = bf16[64,2048]{1,0:T(8,128)(2,1)} copy(bf16[64,2048]{1,0:T(8,128)(2,1)} %get-tuple-element.18) | data formatting | bytes 524288
  60.7 0.0 copy-done
  60.7 0.0 copy-start.3
  60.7 0.6 %copy.27 = bf16[64,512]{1,0:T(8,128)(2,1)} copy(bf16[64,512]{1,0:T(8,128)(2,1)S(1)} %copy-done) | data formatting | bytes 131072
  61.3 0.1 copy-done.3
  61.4 0.6 copy.28
  (2 shorter events, 0.0 us)
Async XLA Ops:
  0.6 0.7 %copy-start.1 = (f32[6,256]{1,0:T(8,128)S(1)}, f32[6,256]{1,0:T(8,128)}, u32[]{:S(2)}) copy-start(f32[6,256]{1,0:T(8,128)} %gain.1) | copy-start | bytes 18436
  0.6 0.7 %copy-start.2 = (f32[6,256]{1,0:T(8,128)S(1)}, f32[6,256]{1,0:T(8,128)}, u32[]{:S(2)}) copy-start(f32[6,256]{1,0:T(8,128)} %shift.1) | copy-start | bytes 18436
  59.0 1.7 %copy-start = (bf16[64,512]{1,0:T(8,128)(2,1)S(1)}, bf16[64,512]{1,0:T(8,128)(2,1)}, u32[]{:S(2)}) copy-start(bf16[64,512]{1,0:T(8,128)(2,1)} %get-tuple-element.19) | copy-start | bytes 196612
  60.7 0.7 %copy-start.3 = (bf16[64,128]{1,0:T(8,128)(2,1)S(1)}, bf16[64,128]{1,0:T(8,128)(2,1)}, u32[]{:S(2)}) copy-start(bf16[64,128]{1,0:T(8,128)(2,1)} %get-tuple-element.20) | copy-start | bytes 49156

commit v2 on v1

--- a/solution.py
+++ b/solution.py
@@ -153,39 +153,42 @@
     return jnp.where(col == edge, 0.0, moved)
 
 
-FEAT, LATW, CONVW, RAISE, COARSE, MOMENT, FINAL = range(7)
-KINDS = 7
+FEAT, RAISE, COARSE, MOMENT, FINAL = range(5)
+KINDS = 5
 
 
 def pyramid_kernel(
     n, bands, rows, cols, neck, half,
-    feat, dw, bias, lat, lc, oc, gain, shift, gcol, scol,
+    feat, dw, bias, lat, lc, oc, gain, shift,
     o8, o16, o32, o64,
     fbuf, dwv, lcv, latw, w0, w1, w2, acc, pool, ubuf, usend, cbuf, v8, x16, x32,
     halo8, halo16, halo32, send8, send16, send32, mbuf, inter, osend,
-    ssem, rsem, lsem, hs, hr,
+    ssem, rsem, lsem, hs, hr, fs, fr, ws, wr,
 ):
     me = lax.axis_index("mp")
     band = lax.axis_index("space")
+    layer = lax.axis_index("dp")
+    layers = lax.axis_size("dp")
     depth = feat.shape[1]
     own = neck // n
     hown = half // n
     px = rows * cols
     prows = rows // n
     part = prows * cols
-    nine = 9 * neck
     r2, c2 = rows // 2, cols // 2
     px2 = r2 * c2
 
     def at_mp(k):
-        return lax.rem(me + k, n)
+        fast = lax.rem(lax.rem(me, 2) + k % 2, 2)
+        slow = lax.rem(lax.div(me, 2) + k // 2, 2)
+        return 2 * slow + fast
 
     locals_ = [
         pltpu.make_async_copy(feat, fbuf.at[0], lsem.at[0]),
         pltpu.make_async_copy(dw, dwv, lsem.at[1]),
         pltpu.make_async_copy(lc, lcv, lsem.at[2]),
         pltpu.make_async_copy(lat, latw.at[pl.ds(pl.multiple_of(me * own, own), own)], lsem.at[3]),
-        pltpu.make_async_copy(oc.at[0], w0.at[pl.ds(pl.multiple_of(me * own, own), own)], lsem.at[4]),
+        pltpu.make_async_copy(oc.at[0], w0.at[:, pl.ds(pl.multiple_of(me * own, own), own)], lsem.at[4]),
         pltpu.make_async_copy(oc.at[1], w1, lsem.at[5]),
         pltpu.make_async_copy(oc.at[2], w2, lsem.at[6]),
     ]
@@ -203,7 +206,11 @@
                 device_id={"space": lax.rem(band + b, bands), "mp": at_mp(k)},
                 device_id_type=MESH,
             )
-    pl.semaphore_wait(barrier, bands * n - 1)
+    for b in range(1, layers):
+        pl.semaphore_signal(
+            barrier, inc=1, device_id={"dp": lax.rem(layer + b, layers)}, device_id_type=MESH
+        )
+    pl.semaphore_wait(barrier, bands * n - 1 + layers - 1)
 
     def remote(src, dst, kind, k):
         return pltpu.make_async_remote_copy(
@@ -225,8 +232,74 @@
             copy.start()
             sends[kind, k] = copy
 
-    launch(FEAT, lambda k: (feat, fbuf.at[k]))
-    launch(LATW, lambda k: (lat, latw.at[mine]))
+    top = pl.ds(0, px // 2)
+    low = pl.ds(px // 2, px // 2)
+
+    def feature_copy(src, dst, slot, half_at, k):
+        return pltpu.make_async_remote_copy(
+            src_ref=src, dst_ref=dst, send_sem=fs.at[slot, half_at],
+            recv_sem=fr.at[slot, half_at], device_id={"mp": at_mp(k)}, device_id_type=MESH)
+
+    first = {}
+    for k, half_at in ((1, 0), (2, 1), (1, 1), (2, 0)):
+        span = (top, low)[half_at]
+        first[k, half_at] = feature_copy(feat.at[span], fbuf.at[k, span], k, half_at, k)
+    first[1, 0].start()
+    first[2, 1].start()
+
+    piece = own // layers
+    taps = oc.shape[1]
+    widths = (neck // bands, half // bands)
+
+    def block(which, src, rows_at, count, ref, own_ref):
+        lanes = pl.ds(pl.multiple_of(band * widths[which], widths[which]), widths[which])
+        base = rows_at if own_ref else src * own + rows_at
+        span = pl.ds(pl.multiple_of(base, count), count)
+        if which == 0:
+            return ref.at[0, :, span, lanes] if own_ref else ref.at[:, span, lanes]
+        return ref.at[span, lanes]
+
+    sources = (oc, lat)
+    targets = (w0, latw)
+    weight_sends = []
+    stage_one, stage_two, stage_three = {}, {}, {}
+    start_rows = layer * piece
+    for which in (1, 0):
+        for k in range(1, n):
+            copy = pltpu.make_async_remote_copy(
+                src_ref=block(which, me, start_rows, piece, sources[which], True),
+                dst_ref=block(which, me, start_rows, piece, targets[which], False),
+                send_sem=ws.at[which, 0, k], recv_sem=wr.at[which, 0, k],
+                device_id={"mp": at_mp(k)}, device_id_type=MESH)
+            copy.start()
+            stage_one[which, k] = copy
+    first[1, 1].start()
+    first[2, 0].start()
+
+    def share_along_dp():
+        for which in (1, 0):
+            for k in range(1, n):
+                stage_one[which, k].wait_recv()
+                for step in range(1, layers):
+                    here = block(which, at_mp(k), start_rows, piece, targets[which], False)
+                    copy = pltpu.make_async_remote_copy(
+                        src_ref=here, dst_ref=here,
+                        send_sem=ws.at[which, step, k], recv_sem=wr.at[which, step, k],
+                        device_id={"dp": lax.rem(layer + step, layers)}, device_id_type=MESH)
+                    copy.start()
+                    stage_two[which, k, step] = copy
+
+    def share_with_core(which):
+        for k in range(1, n):
+            for step in range(1, layers):
+                stage_two[which, k, step].wait_recv()
+            here = block(which, at_mp(k), 0, own, targets[which], False)
+            copy = pltpu.make_async_remote_copy(
+                src_ref=here, dst_ref=here,
+                send_sem=ws.at[which, layers, k], recv_sem=wr.at[which, layers, k],
+                device_id={"space": lax.rem(band + 1, bands)}, device_id_type=MESH)
+            copy.start()
+            stage_three[which, k] = copy
 
     lat16 = jnp.zeros((own, px), jnp.float32)
     lat32 = jnp.zeros((own, px2), jnp.float32)
@@ -234,18 +307,30 @@
         if k == 0:
             for i in range(3):
                 locals_[i].wait()
+        elif k == 1:
+            first[1, 0].wait_recv()
+            relay = [feature_copy(fbuf.at[1, top], fbuf.at[3, top], 3, 0, 2)]
+            relay[0].start()
+            first[2, 1].wait_recv()
+            relay.append(feature_copy(fbuf.at[2, low], fbuf.at[3, low], 3, 1, 1))
+            relay[1].start()
+            first[1, 1].wait_recv()
+        elif k == 2:
+            first[2, 0].wait_recv()
         else:
-            sends[FEAT, k].wait_recv()
-        src = lax.rem(me - k + n, n)
+            share_along_dp()
+            relay[0].wait_recv()
+            relay[1].wait_recv()
+        src = at_mp(k)
         span = pl.ds(pl.multiple_of(src * depth, depth), depth)
-        block = fbuf[k]
-        term = nt(block, dwv[:, span])
+        values = fbuf[k]
+        term = nt(values, dwv[:, span])
         if k == 0:
             acc[...] = term
         else:
             acc[...] += term
-        lat16 = lat16 + nt(lcv[0:own, span], block)
-        floats = block.astype(jnp.float32).reshape(r2, 2 * cols, depth)
+        lat16 = lat16 + nt(lcv[0:own, span], values)
+        floats = values.astype(jnp.float32).reshape(r2, 2 * cols, depth)
         tall = jnp.maximum(floats[:, :cols], floats[:, cols:]).reshape(r2 * cols, depth)
         halves = []
         for g in range(depth // 128):
@@ -267,16 +352,15 @@
     cbuf[mine, 0:px] = lat16.astype(jnp.bfloat16)
     cbuf[mine, px:] = lat32.astype(jnp.bfloat16)
     launch(COARSE, lambda k: (cbuf.at[mine], cbuf.at[mine]))
-    locals_[4].wait()
-    launch(CONVW, lambda k: (oc.at[0], w0.at[mine]))
+    share_with_core(1)
 
     locals_[3].wait()
     for k in peers:
-        sends[LATW, k].wait_recv()
+        stage_three[1, k].wait_recv()
     total = nt(usend[me], latw[:, pl.ds(pl.multiple_of(me * hown, hown), hown)])
     for k in peers:
         sends[RAISE, k].wait_recv()
-        src = lax.rem(me - k + n, n)
+        src = at_mp(k)
         total = total + nt(ubuf[k], latw[:, pl.ds(pl.multiple_of(src * hown, hown), hown)])
     own_rows = 2 * prows
     wide = own_rows * cols
@@ -351,6 +435,7 @@
 
     fill8(cols, wide, zero, one)
 
+    share_with_core(0)
     for k in peers:
         sends[COARSE, k].wait_recv()
     coarse = cbuf[...].astype(jnp.float32).T
@@ -386,7 +471,7 @@
         for tap in range(9):
             r, q = tap // 3, tap % 3
             result = result + nt(
-                w[:, tap * neck : (tap + 1) * neck], x[q, r * width : (r + height) * width, :]
+                w[tap], x[q, r * width : (r + height) * width, :]
             )
         result = result.astype(jnp.bfloat16).astype(jnp.float32)
         span = slice(at, at + height * width)
@@ -398,14 +483,15 @@
     finish8()
     fill8(0, cols, halo8[0, 0:cols].astype(jnp.float32), halo8[0, cols:].astype(jnp.float32))
     fill8(cols + wide, cols, halo8[1, 0:cols].astype(jnp.float32), halo8[1, cols:].astype(jnp.float32))
+    locals_[4].wait()
     for k in peers:
-        sends[CONVW, k].wait_recv()
+        stage_three[0, k].wait_recv()
     for b in range(2):
         result = jnp.zeros((wide, neck), jnp.float32)
         for tap in range(9):
             r, q = tap // 3, tap % 3
             result = result + nt(
-                v8[b + q, r * cols : r * cols + wide, :], w0[:, tap * neck : (tap + 1) * neck]
+                v8[b + q, r * cols : r * cols + wide, :], w0[tap]
             )
         out = lane_norm(result.astype(jnp.bfloat16), gain[1:2, :], shift[1:2, :])
         for g in range(neck // 128):
@@ -415,6 +501,15 @@
     cells = pl.ds(pl.multiple_of(me * 2 * wide, 2 * wide), 2 * wide)
     launch(FINAL, lambda k: (osend.at[pl.ds(pl.multiple_of(at_mp(k) * own, own), own)], o8.at[:, cells]))
     o8[:, cells] = osend[mine, :]
+
+    lane = lax.broadcasted_iota(jnp.int32, (own, neck), 1)
+    row = lax.broadcasted_iota(jnp.int32, (own, neck), 0)
+    chosen = lane == row + me * own
+
+    def own_column(table, index):
+        return jnp.sum(
+            jnp.where(chosen, table[index : index + 1, :], 0.0), axis=1, keepdims=True
+        )
 
     for k in peers:
         sends[MOMENT, k].wait_recv()
@@ -427,20 +522,24 @@
         center = moments[0:1, span]
         spread = moments[1:2, span] - center * center
         scaled = (result - center) * lax.rsqrt(spread + EPSILON)
-        final = (scaled * gcol[:, level : level + 1] + scol[:, level : level + 1]).astype(jnp.bfloat16)
+        final = (
+            scaled * own_column(gain, 2 * level + 1) + own_column(shift, 2 * level + 1)
+        ).astype(jnp.bfloat16)
         if level == 1:
             o16[...] = final
         else:
             o32[...] = final
-            count = o64.shape[1]
+            count = o64.shape[0]
             wide2 = c2 // 2
-            cell = lax.broadcasted_iota(jnp.int32, (px2, count), 0)
-            target = lax.broadcasted_iota(jnp.int32, (px2, count), 1)
+            cell = lax.broadcasted_iota(jnp.int32, (count, px2), 1)
+            target = lax.broadcasted_iota(jnp.int32, (count, px2), 0)
             wanted = lax.div(target, wide2) * (2 * c2) + 2 * lax.rem(target, wide2)
             pick = jnp.where(cell == wanted, 1.0, 0.0).astype(jnp.bfloat16)
-            o64[...] = jnp.dot(final, pick, preferred_element_type=jnp.float32).astype(jnp.bfloat16)
-
-    for kind in range(KINDS):
+            o64[...] = nt(pick, final).astype(jnp.bfloat16)
+
+    for copy in (*first.values(), *relay, *stage_one.values(), *stage_two.values(), *stage_three.values()):
+        copy.wait_send()
+    for kind in (RAISE, COARSE, MOMENT, FINAL):
         for k in peers:
             sends[kind, k].wait_send()
     for k in peers:
@@ -456,17 +555,15 @@
     hown = deconv_weight.shape[1]
     own = lateral_eight.shape[0]
     neck, half = own * n, hown * n
+    layers = lax.axis_size("dp")
     px, px2 = rows * cols, rows * cols // 4
     wide = 2 * (rows // n) * cols
-    first = lax.axis_index("mp") * own
-    gcol = lax.dynamic_slice_in_dim(norm_gain[1::2], first, own, 1).T
-    scol = lax.dynamic_slice_in_dim(norm_shift[1::2], first, own, 1).T
     bf, f32 = jnp.bfloat16, jnp.float32
     vmem = pl.BlockSpec(memory_space=pltpu.VMEM)
     hbm = pl.BlockSpec(memory_space=pl.ANY)
     shapes = [
         ((n, px, depth), bf), ((4 * hown, full), bf), ((2 * own, full), bf),
-        ((neck, half), bf), ((neck, 9 * neck), bf), ((own, 9 * neck), bf), ((own, 9 * neck), bf),
+        ((neck, half), bf), ((9, neck, neck), bf), ((9, own, neck), bf), ((9, own, neck), bf),
         ((px, 4 * hown), f32), ((px // 2, 128), f32), ((n, 2 * wide, hown), bf),
         ((n, 2 * wide, hown), bf), ((neck, px + px2), bf),
         ((4, wide + 2 * cols, neck), bf), ((3, px + 2 * cols, neck), bf),
@@ -475,18 +572,20 @@
         ((2, 2 * cols, neck), bf), ((2, cols, neck), bf), ((2, cols // 2, neck), bf),
         ((n, 8, px + px2), f32), ((neck // 128, 2 * wide, 128), f32), ((neck, 2 * wide), bf),
     ]
-    return pl.pallas_call(
+    eight, sixteen, thirty, sixty = pl.pallas_call(
         functools.partial(pyramid_kernel, n, bands, rows, cols, neck, half),
         out_shape=[
             jax.ShapeDtypeStruct((own, 4 * px), bf), jax.ShapeDtypeStruct((own, px), bf),
-            jax.ShapeDtypeStruct((own, px2), bf), jax.ShapeDtypeStruct((own, px2 // 4), bf),
+            jax.ShapeDtypeStruct((own, px2), bf), jax.ShapeDtypeStruct((px2 // 4, own), bf),
         ],
-        in_specs=[hbm, hbm, vmem, hbm, hbm, hbm, vmem, vmem, vmem, vmem],
+        in_specs=[hbm, hbm, vmem, hbm, hbm, hbm, vmem, vmem],
         out_specs=[vmem] * 4,
         scratch_shapes=[pltpu.VMEM(s, d) for s, d in shapes] + [
             pltpu.SemaphoreType.DMA((KINDS, n)), pltpu.SemaphoreType.DMA((KINDS, n)),
             pltpu.SemaphoreType.DMA((7,)), pltpu.SemaphoreType.DMA((3, 2)),
             pltpu.SemaphoreType.DMA((3, 2)),
+            pltpu.SemaphoreType.DMA((n, 2)), pltpu.SemaphoreType.DMA((n, 2)),
+            pltpu.SemaphoreType.DMA((2, layers + 1, n)), pltpu.SemaphoreType.DMA((2, layers + 1, n)),
         ],
         compiler_params=pltpu.CompilerParams(
             collective_id=0, has_side_effects=True, vmem_limit_bytes=56 << 20
@@ -494,14 +593,18 @@
     )(
         features.reshape(px, depth), deconv_weight.reshape(4 * hown, full),
         deconv_bias.reshape(1, hown), lateral_eight, lateral_coarse.reshape(2 * own, full),
-        output_conv.reshape(3, own, 9 * neck), norm_gain, norm_shift, gcol, scol,
-    )
+        output_conv.transpose(0, 2, 1, 3), norm_gain, norm_shift,
+    )
+    return eight, sixteen, thirty, sixty.T
 
 
 def per_device(features, deconv_weight, *rest):
     n = lax.axis_size("mp")
     rows, cols, depth = features.shape
     aligned = depth % 128 == 0 and deconv_weight.shape[1] % 128 == 0
+    bands, layers = lax.axis_size("space"), lax.axis_size("dp")
+    own, neck = rest[1].shape[0], rest[3].shape[3]
+    aligned = aligned and n == 4 and bands == 2 and own % (16 * layers) == 0 and neck % (128 * bands) == 0
     if aligned and rows % n == 0 and rows % 4 == 0 and cols % 64 == 0:
         return tuple(fused(features, deconv_weight, *rest))
     return channel_pyramid(features, deconv_weight, *rest)

time: 62.5 us -> 47.2 us (0.76)
  Pallas kernels: 52.6 us -> 42.5 us
  local copies, waits for them, and re-layouts: 8.78 us -> 3.72 us
    pallas_call x1, Pallas kernels: 52.6 us -> 42.5 us  [fused(): pl.pallas_call(functools.partial(pyramid_kernel, n, bands, rows, cols, ne...]
    reshape x1 -> x0, local copies, waits for them, and re-layouts: 2.14 us -> none  [fused(): output_conv.reshape(3, own, 9 * neck)]
    unnamed x13 -> x10, local copies, waits for them, and re-layouts: 5.13 us -> 3.72 us
    pallas_call x1 -> x0, local copies, waits for them, and re-layouts: 1.39 us -> none  [fused(): pl.pallas_call(functools.partial(pyramid_kernel, n, bands, rows, cols, ne...]
where the time goes in v2:
time: 47.2 us; the launch traced here: 46.8 us
  Pallas kernels  42.5 us (90%)
  local copies, waits for them, and re-layouts  3.72 us (8%)
  between operations  0.65 us (1%)
    pallas_call x1, Pallas kernels, fused(): pl.pallas_call(functools.partial(pyramid_kernel, n, bands, rows, cols, ne...  42.5 us
    unnamed x10, local copies, waits for them, and re-layouts  3.72 us

profile of v2, /device:TPU:0, one launch (start us, length us, event | category | flops | bytes accessed | tf_op | source)
XLA Modules:
  0.0 46.8 jit_solution(4981512901295540326)
XLA Ops:
  0.6 42.5 %shard_map.111 = (bf16[64,2048]{1,0:T(8,128)(2,1)}, bf16[64,512]{1,0:T(8,128)(2,1)}, bf16[64,128]{1,0:T(8,128)(2,1)}, bf16[32,64]{1,0:T(8,128)(2,1)}) custom-call(bf16[512,256]{1,0:T(8,128)(2,1)} %bitcast.8, bf16[512,1024]{1,0:T(8,128)(2,1)} %bitcast.6, f32[1,128]{1,0:T(1,128)} %bitcast.11, bf16[64,512]{1,0:T(8,128)(2,1)} %lat.1, bf16[128,1024]{1,0:T(8,128)(2,1)} %bitcast.9, ...), custom_call_target="tpu_custom_call" | custom-call | tf_op jit(solution)/shard_map/pallas_call | solution.py:575
  43.1 0.0 copy-start
  43.1 1.7 %copy.16 = bf16[64,2048]{1,0:T(8,128)(2,1)} copy(bf16[64,2048]{1,0:T(8,128)(2,1)} %get-tuple-element.16) | data formatting | bytes 524288
  44.8 0.0 copy-done
  44.8 0.0 copy-start.1
  44.8 0.6 %copy.17 = bf16[64,512]{1,0:T(8,128)(2,1)} copy(bf16[64,512]{1,0:T(8,128)(2,1)S(1)} %copy-done) | data formatting | bytes 131072
  45.4 0.1 copy-done.1
  45.5 0.0 copy-start.2
  45.5 0.6 %copy.18 = bf16[64,128]{1,0:T(8,128)(2,1)} copy(bf16[64,128]{1,0:T(8,128)(2,1)S(1)} %copy-done.1) | data formatting | bytes 32768
  46.1 0.1 copy-done.2
  46.2 0.6 %copy.19 = bf16[64,32]{0,1:T(8,128)(2,1)} copy(bf16[64,32]{0,1:T(8,128)(2,1)S(1)} %bitcast.10) | data formatting | bytes 8192
Async XLA Ops:
  43.1 1.7 %copy-start = (bf16[64,512]{1,0:T(8,128)(2,1)S(1)}, bf16[64,512]{1,0:T(8,128)(2,1)}, u32[]{:S(2)}) copy-start(bf16[64,512]{1,0:T(8,128)(2,1)} %get-tuple-element.17) | copy-start | bytes 196612
  44.8 0.7 %copy-start.1 = (bf16[64,128]{1,0:T(8,128)(2,1)S(1)}, bf16[64,128]{1,0:T(8,128)(2,1)}, u32[]{:S(2)}) copy-start(bf16[64,128]{1,0:T(8,128)(2,1)} %get-tuple-element.18) | copy-start | bytes 49156
  45.5 0.7 %copy-start.2 = (bf16[32,64]{1,0:T(8,128)(2,1)S(1)}, bf16[32,64]{1,0:T(8,128)(2,1)}, u32[]{:S(2)}) copy-start(bf16[32,64]{1,0:T(8,128)(2,1)} %get-tuple-element.11) | copy-start | bytes 12292

commit v3 on v2

--- a/solution.py
+++ b/solution.py
@@ -153,8 +153,8 @@
     return jnp.where(col == edge, 0.0, moved)
 
 
-FEAT, RAISE, COARSE, MOMENT, FINAL = range(5)
-KINDS = 5
+RAISE, COARSE, MOMENT, FINAL = range(4)
+KINDS = FINAL + 2
 
 
 def pyramid_kernel(
@@ -460,6 +460,40 @@
             band > 0, {"space": jnp.maximum(band - 1, 0)},
             band < bands - 1, {"space": jnp.minimum(band + 1, bands - 1)},
         ))
+    finish8()
+    fill8(0, cols, halo8[0, 0:cols].astype(jnp.float32), halo8[0, cols:].astype(jnp.float32))
+    fill8(cols + wide, cols, halo8[1, 0:cols].astype(jnp.float32), halo8[1, cols:].astype(jnp.float32))
+    locals_[4].wait()
+    for k in peers:
+        stage_three[0, k].wait_recv()
+    part_px = wide // 2
+    for part_at in range(2):
+        result = jnp.zeros((2 * part_px, neck), jnp.float32)
+        for tap in range(9):
+            r, q = tap // 3, tap % 3
+            at = r * cols + part_at * part_px
+            window = v8[q : q + 2, at : at + part_px, :].reshape(2 * part_px, neck)
+            result = result + nt(window, w0[tap])
+        out = lane_norm(result.astype(jnp.bfloat16), gain[1:2, :], shift[1:2, :])
+        for g in range(neck // 128):
+            for b in range(2):
+                inter[g, pl.ds(2 * part_at * part_px + b, part_px, stride=2), :] = out[
+                    b * part_px : (b + 1) * part_px, g * 128 : (g + 1) * 128
+                ]
+        for g in range(neck // 128):
+            osend[part_at, g * 128 : (g + 1) * 128, :] = inter[
+                g, part_at * wide : (part_at + 1) * wide, :
+            ].T.astype(jnp.bfloat16)
+        cells = pl.ds(pl.multiple_of((2 * me + part_at) * wide, wide), wide)
+        launch(
+            FINAL + part_at,
+            lambda k: (
+                osend.at[part_at, pl.ds(pl.multiple_of(at_mp(k) * own, own), own)],
+                o8.at[:, cells],
+            ),
+        )
+        o8[:, cells] = osend[part_at, mine, :]
+
     maps = []
     locals_[5].wait()
     locals_[6].wait()
@@ -479,28 +513,6 @@
         mbuf[0, 1:2, span] = jnp.sum(result * result, axis=0, keepdims=True)
         maps.append(result)
     launch(MOMENT, lambda k: (mbuf.at[0], mbuf.at[k]))
-
-    finish8()
-    fill8(0, cols, halo8[0, 0:cols].astype(jnp.float32), halo8[0, cols:].astype(jnp.float32))
-    fill8(cols + wide, cols, halo8[1, 0:cols].astype(jnp.float32), halo8[1, cols:].astype(jnp.float32))
-    locals_[4].wait()
-    for k in peers:
-        stage_three[0, k].wait_recv()
-    for b in range(2):
-        result = jnp.zeros((wide, neck), jnp.float32)
-        for tap in range(9):
-            r, q = tap // 3, tap % 3
-            result = result + nt(
-                v8[b + q, r * cols : r * cols + wide, :], w0[tap]
-            )
-        out = lane_norm(result.astype(jnp.bfloat16), gain[1:2, :], shift[1:2, :])
-        for g in range(neck // 128):
-            inter[g, pl.ds(b, wide, stride=2), :] = out[:, g * 128 : (g + 1) * 128]
-    for g in range(neck // 128):
-        osend[g * 128 : (g + 1) * 128, :] = inter[g].T.astype(jnp.bfloat16)
-    cells = pl.ds(pl.multiple_of(me * 2 * wide, 2 * wide), 2 * wide)
-    launch(FINAL, lambda k: (osend.at[pl.ds(pl.multiple_of(at_mp(k) * own, own), own)], o8.at[:, cells]))
-    o8[:, cells] = osend[mine, :]
 
     lane = lax.broadcasted_iota(jnp.int32, (own, neck), 1)
     row = lax.broadcasted_iota(jnp.int32, (own, neck), 0)
@@ -539,11 +551,18 @@
 
     for copy in (*first.values(), *relay, *stage_one.values(), *stage_two.values(), *stage_three.values()):
         copy.wait_send()
-    for kind in (RAISE, COARSE, MOMENT, FINAL):
+    for kind in range(KINDS):
         for k in peers:
             sends[kind, k].wait_send()
     for k in peers:
         sends[FINAL, k].wait_recv()
+        sends[FINAL + 1, k].wait_recv()
+
+
+def hand_over(*refs):
+    count = len(refs) // 2
+    for source, target in zip(refs[:count], refs[count:]):
+        target[...] = source[...]
 
 
 def fused(features, deconv_weight, deconv_bias, lateral_eight, lateral_coarse, output_conv,
@@ -570,9 +589,9 @@
         ((3, px2 + cols, neck), bf),
         ((2, 2 * cols, neck), bf), ((2, cols, neck), bf), ((2, cols // 2, neck), bf),
         ((2, 2 * cols, neck), bf), ((2, cols, neck), bf), ((2, cols // 2, neck), bf),
-        ((n, 8, px + px2), f32), ((neck // 128, 2 * wide, 128), f32), ((neck, 2 * wide), bf),
+        ((n, 8, px + px2), f32), ((neck // 128, 2 * wide, 128), f32), ((2, neck, wide), bf),
     ]
-    eight, sixteen, thirty, sixty = pl.pallas_call(
+    results = pl.pallas_call(
         functools.partial(pyramid_kernel, n, bands, rows, cols, neck, half),
         out_shape=[
             jax.ShapeDtypeStruct((own, 4 * px), bf), jax.ShapeDtypeStruct((own, px), bf),
@@ -595,6 +614,12 @@
         deconv_bias.reshape(1, hown), lateral_eight, lateral_coarse.reshape(2 * own, full),
         output_conv.transpose(0, 2, 1, 3), norm_gain, norm_shift,
     )
+    eight, sixteen, thirty, sixty = pl.pallas_call(
+        hand_over,
+        out_shape=[jax.ShapeDtypeStruct(r.shape, r.dtype) for r in results],
+        in_specs=[vmem] * 4,
+        out_specs=[vmem] * 4,
+    )(*results)
     return eight, sixteen, thirty, sixty.T
 
 

time: 47.2 us -> 44.5 us (0.943)
  local copies, waits for them, and re-layouts: 3.72 us -> 0 us
  Pallas kernels: 42.5 us -> 43.6 us
    unnamed x10 -> x0, local copies, waits for them, and re-layouts: 3.72 us -> none
    pallas_call x0 -> x1, Pallas kernels: none -> 1.73 us  [fused(): pl.pallas_call(hand_over, out_shape=[jax.ShapeDtypeStruct(r.shape, r.dtyp...]
    pallas_call x1, Pallas kernels: 42.5 us -> 41.9 us  [fused(): pl.pallas_call(functools.partial(pyramid_kernel, n, bands, rows, cols, ne...]
where the time goes in v3:
time: 44.5 us; the launch traced here: 44.3 us
  Pallas kernels  43.6 us (98%)
  between operations  0.64 us (1%)
    pallas_call x1, Pallas kernels, fused(): pl.pallas_call(functools.partial(pyramid_kernel, n, bands, rows, cols, ne...  41.9 us
    pallas_call x1, Pallas kernels, fused(): pl.pallas_call(hand_over, out_shape=[jax.ShapeDtypeStruct(r.shape, r.dtyp...  1.73 us

profile of v3, /device:TPU:0, one launch (start us, length us, event | category | flops | bytes accessed | tf_op | source)
XLA Modules:
  0.0 44.3 jit_solution(13787159190985487890)
XLA Ops:
  0.6 41.9 %shard_map.111 = (bf16[64,2048]{1,0:T(8,128)(2,1)}, bf16[64,512]{1,0:T(8,128)(2,1)}, bf16[64,128]{1,0:T(8,128)(2,1)}, bf16[32,64]{1,0:T(8,128)(2,1)}) custom-call(bf16[512,256]{1,0:T(8,128)(2,1)} %bitcast.8, bf16[512,1024]{1,0:T(8,128)(2,1)} %bitcast.6, f32[1,128]{1,0:T(1,128)} %bitcast.10, bf16[64,512]{1,0:T(8,128)(2,1)} %lat.1, bf16[128,1024]{1,0:T(8,128)(2,1)} %bitcast.9, ...), custom_call_target="tpu_custom_call" | custom-call | tf_op jit(solution)/shard_map/pallas_call | solution.py:594
  42.5 1.7 %shard_map.112 = (bf16[64,2048]{1,0:T(8,128)(2,1)}, bf16[64,512]{1,0:T(8,128)(2,1)}, bf16[64,128]{1,0:T(8,128)(2,1)}, bf16[32,64]{1,0:T(8,128)(2,1)}) custom-call(bf16[64,2048]{1,0:T(8,128)(2,1)} %get-tuple-element.12.refs_0_, bf16[64,512]{1,0:T(8,128)(2,1)} %get-tuple-element.13.refs_1_, bf16[64,128]{1,0:T(8,128)(2,1)} %get-tuple-element.14.refs_2_, ...), custom_call_target="tpu_custom_call" | custom-call | tf_op jit(solution)/shard_map/pallas_call | solution.py:617

commit v4 on v3

--- a/solution.py
+++ b/solution.py
@@ -303,6 +303,24 @@
 
     lat16 = jnp.zeros((own, px), jnp.float32)
     lat32 = jnp.zeros((own, px2), jnp.float32)
+
+    def span_of(k):
+        return pl.ds(pl.multiple_of(at_mp(k) * depth, depth), depth)
+
+    def laterals(k, sixteen, thirty):
+        span = span_of(k)
+        values = fbuf[k]
+        floats = values.astype(jnp.float32).reshape(r2, 2 * cols, depth)
+        tall = jnp.maximum(floats[:, :cols], floats[:, cols:]).reshape(r2 * cols, depth)
+        halves = []
+        for g in range(depth // 128):
+            pool[...] = tall[:, g * 128 : (g + 1) * 128]
+            halves.append(
+                jnp.maximum(pool[pl.ds(0, px2, stride=2), :], pool[pl.ds(1, px2, stride=2), :])
+            )
+        pooled = jnp.concatenate(halves, axis=1).astype(jnp.bfloat16)
+        return sixteen + nt(lcv[0:own, span], values), thirty + nt(lcv[own:, span], pooled)
+
     for k in range(n):
         if k == 0:
             for i in range(3):
@@ -314,41 +332,38 @@
             first[2, 1].wait_recv()
             relay.append(feature_copy(fbuf.at[2, low], fbuf.at[3, low], 3, 1, 1))
             relay[1].start()
+            share_along_dp()
             first[1, 1].wait_recv()
         elif k == 2:
             first[2, 0].wait_recv()
         else:
-            share_along_dp()
             relay[0].wait_recv()
             relay[1].wait_recv()
-        src = at_mp(k)
-        span = pl.ds(pl.multiple_of(src * depth, depth), depth)
-        values = fbuf[k]
-        term = nt(values, dwv[:, span])
+        if k == n - 1:
+            break
         if k == 0:
-            acc[...] = term
+            acc[...] = nt(fbuf[k], dwv[:, span_of(k)])
         else:
-            acc[...] += term
-        lat16 = lat16 + nt(lcv[0:own, span], values)
-        floats = values.astype(jnp.float32).reshape(r2, 2 * cols, depth)
-        tall = jnp.maximum(floats[:, :cols], floats[:, cols:]).reshape(r2 * cols, depth)
-        halves = []
-        for g in range(depth // 128):
-            pool[...] = tall[:, g * 128 : (g + 1) * 128]
-            halves.append(jnp.maximum(pool[pl.ds(0, px2, stride=2), :], pool[pl.ds(1, px2, stride=2), :]))
-        pooled = jnp.concatenate(halves, axis=1).astype(jnp.bfloat16)
-        lat32 = lat32 + nt(lcv[own:, span], pooled)
-
-    for d in range(n):
+            acc[...] += nt(fbuf[k], dwv[:, span_of(k)])
+        lat16, lat32 = laterals(k, lat16, lat32)
+
+    for k in (3, 1, 2, 0):
+        rows_at = pl.ds(pl.multiple_of(at_mp(k) * part, part), part)
+        raised = acc[rows_at, :] + nt(fbuf[n - 1, rows_at, :], dwv[:, span_of(n - 1)])
         for il in range(prows):
-            base = (d * prows + il) * cols
             for a in range(2):
                 for b in range(2):
                     tap = 2 * a + b
-                    value = acc[base : base + cols, tap * hown : (tap + 1) * hown] + bias[...]
+                    value = raised[
+                        il * cols : (il + 1) * cols, tap * hown : (tap + 1) * hown
+                    ] + bias[...]
                     at = (b * 2 * prows + 2 * il + a) * cols
-                    usend[d, at : at + cols, :] = value.astype(jnp.bfloat16)
-    launch(RAISE, lambda k: (usend.at[at_mp(k)], ubuf.at[k]))
+                    usend[k, at : at + cols, :] = value.astype(jnp.bfloat16)
+        if k > 0:
+            copy = remote(usend.at[k], ubuf.at[k], RAISE, k)
+            copy.start()
+            sends[RAISE, k] = copy
+    lat16, lat32 = laterals(n - 1, lat16, lat32)
     cbuf[mine, 0:px] = lat16.astype(jnp.bfloat16)
     cbuf[mine, px:] = lat32.astype(jnp.bfloat16)
     launch(COARSE, lambda k: (cbuf.at[mine], cbuf.at[mine]))
@@ -357,7 +372,7 @@
     locals_[3].wait()
     for k in peers:
         stage_three[1, k].wait_recv()
-    total = nt(usend[me], latw[:, pl.ds(pl.multiple_of(me * hown, hown), hown)])
+    total = nt(usend[0], latw[:, pl.ds(pl.multiple_of(me * hown, hown), hown)])
     for k in peers:
         sends[RAISE, k].wait_recv()
         src = at_mp(k)

time: 44.5 us -> 44.2 us (level)
  no operation moved by 1% of the time
where the time goes in v4:
time: 44.2 us; the launch traced here: 44 us
  Pallas kernels  43.3 us (98%)
  between operations  0.64 us (1%)
    pallas_call x1, Pallas kernels, fused(): pl.pallas_call(functools.partial(pyramid_kernel, n, bands, rows, cols, ne...  41.6 us
    pallas_call x1, Pallas kernels, fused(): pl.pallas_call(hand_over, out_shape=[jax.ShapeDtypeStruct(r.shape, r.dtyp...  1.73 us

profile of v4, /device:TPU:0, one launch (start us, length us, event | category | flops | bytes accessed | tf_op | source)
XLA Modules:
  0.0 44.0 jit_solution(15158359022924410061)
XLA Ops:
  0.6 41.6 %shard_map.111 = (bf16[64,2048]{1,0:T(8,128)(2,1)}, bf16[64,512]{1,0:T(8,128)(2,1)}, bf16[64,128]{1,0:T(8,128)(2,1)}, bf16[32,64]{1,0:T(8,128)(2,1)}) custom-call(bf16[512,256]{1,0:T(8,128)(2,1)} %bitcast.8, bf16[512,1024]{1,0:T(8,128)(2,1)} %bitcast.6, f32[1,128]{1,0:T(1,128)} %bitcast.10, bf16[64,512]{1,0:T(8,128)(2,1)} %lat.1, bf16[128,1024]{1,0:T(8,128)(2,1)} %bitcast.9, ...), custom_call_target="tpu_custom_call" | custom-call | tf_op jit(solution)/shard_map/pallas_call | solution.py:609
  42.2 1.7 %shard_map.112 = (bf16[64,2048]{1,0:T(8,128)(2,1)}, bf16[64,512]{1,0:T(8,128)(2,1)}, bf16[64,128]{1,0:T(8,128)(2,1)}, bf16[32,64]{1,0:T(8,128)(2,1)}) custom-call(bf16[64,2048]{1,0:T(8,128)(2,1)} %get-tuple-element.12.refs_0_, bf16[64,512]{1,0:T(8,128)(2,1)} %get-tuple-element.13.refs_1_, bf16[64,128]{1,0:T(8,128)(2,1)} %get-tuple-element.14.refs_2_, ...), custom_call_target="tpu_custom_call" | custom-call | tf_op jit(solution)/shard_map/pallas_call | solution.py:632
